TPU v7x, 32 devices: a whole 2x2x4 slice. The times are simulated.
32 devices in a mesh: attn: 8 (over z, x), expert: 4 (over y, core).
Axes of the slice: x: 2, y: 2, z: 4, core: 2. Of those that a mesh axis runs over, the one named last changes fastest.
Arguments:
- resid: bfloat16 [512, 6144], P('attn', 'expert')
- query: bfloat16 [512, 6144], P('attn', 'expert'), may hold values from -1 to 1
- key_cache: bfloat16 [512, 8, 128, 128], P('attn', 'expert'), may hold values from -4 to 4
- value_cache: bfloat16 [512, 8, 128, 128], P('attn', 'expert'), may hold values from -6 to 6
- new_key: bfloat16 [512, 1024], P('attn', 'expert'), may hold values from -4 to 4
- new_value: bfloat16 [512, 1024], P('attn', 'expert'), may hold values from -6 to 6
- lengths: int32 [512], P('attn'), may hold values from 1 to 128, as said below
- norm_gain: float32 [6144], P('expert'), may hold values from 0.1 to 1.9
- router_weight: float32 [6144, 8], P('expert'), may hold values from -0.078125 to 0.078125
- expert_ids: int32 [512, 2], P('attn'), may hold values from 0 to 7, as said below
- w_gate: bfloat16 [8, 6144, 8192], P('expert', None, 'attn'), may hold values from -0.078125 to 0.078125
- w_up: bfloat16 [8, 6144, 8192], P('expert', None, 'attn'), may hold values from -0.078125 to 0.078125
- w_down: bfloat16 [8, 8192, 6144], P('expert', 'attn'), may hold values from -0.0625 to 0.0625
Outputs:
- layer_out: bfloat16 [512, 6144], P('attn', 'expert')
Inputs may be any that keep to these rules, and one draw needn't show every extreme that they name: `expert_ids`: each row names two different experts. Within each aligned block of 64 rows (the rows of one index of attn) no expert is named by more than 32 rows, and one expert, the same in every block, is named by exactly 32 rows in each block. `lengths`: some row has all 128 positions filled and some row has one.
All inputs are finite; a program needn't handle non-finite values.
Results may differ from a plain program's by a relative error of at most 0.0095.
Values may be sent and summed in bfloat16 or wider, within the bound.
A program may use at most 128 MiB of HBM per device.

v0:
```python
import math
import jax
import jax.numpy as jnp
from jax import lax
from jax.sharding import PartitionSpec as P

D = 6144
E = 8
CAP = 32
EPSILON = 1e-05


def on_device(
    resid,
    query,
    key_cache,
    value_cache,
    new_key,
    new_value,
    lengths,
    norm_gain,
    router_weight,
    expert_ids,
    w_gate,
    w_up,
    w_down,
):
    row_count = resid.shape[0]
    width_local = resid.shape[1]
    kv_local = key_cache.shape[1]
    cache_slots = key_cache.shape[2]
    head_size = key_cache.shape[3]
    group_size = query.shape[1] // (kv_local * head_size)
    local_experts = w_gate.shape[0]
    expert_devices = lax.axis_size("expert")
    score_scale = 1.0 / math.sqrt(head_size)
    queries = query.reshape(row_count, kv_local, group_size, head_size)
    scores = (
        jnp.einsum("rkgd,rkld->rkgl", queries, key_cache, preferred_element_type=jnp.float32)
        * score_scale
    )
    fresh_score = (
        jnp.einsum(
            "rkgd,rkd->rkg",
            queries,
            new_key.reshape(row_count, kv_local, head_size),
            preferred_element_type=jnp.float32,
        )
        * score_scale
    )
    usable = lax.broadcasted_iota(jnp.int32, (row_count, cache_slots), 1) < lengths[:, None]
    powers = jnp.where(usable[:, None, None, :], jnp.exp(scores), jnp.float32(0.0))
    fresh_power = jnp.exp(fresh_score)
    denominator = jnp.sum(powers, axis=-1) + fresh_power
    weights_cache = (powers / denominator[..., None]).astype(jnp.bfloat16)
    weight_fresh = (fresh_power / denominator).astype(jnp.bfloat16)
    attended = jnp.einsum(
        "rkgl,rkld->rkgd", weights_cache, value_cache, preferred_element_type=jnp.float32
    )
    attended = attended + weight_fresh.astype(jnp.float32)[..., None] * new_value.astype(
        jnp.float32
    ).reshape(row_count, kv_local, 1, head_size)
    hidden_state = resid.astype(jnp.float32) + attended.reshape(row_count, width_local)
    total_square = lax.psum(jnp.sum(hidden_state * hidden_state, axis=1), "expert")
    normed = hidden_state * lax.rsqrt(total_square / D + EPSILON)[:, None] * norm_gain
    logits = lax.psum(jnp.dot(normed, router_weight, precision=lax.Precision.HIGHEST), "expert")
    narrow = normed.astype(jnp.bfloat16)
    choose = expert_ids[:, :, None] == lax.broadcasted_iota(jnp.int32, (1, 1, E), 2)
    picked = jnp.sum(jnp.where(choose, logits[:, None, :], jnp.float32(0.0)), axis=2)
    first_weight = 1.0 / (1.0 + jnp.exp(picked[:, 1] - picked[:, 0]))
    second_weight = 1.0 / (1.0 + jnp.exp(picked[:, 0] - picked[:, 1]))
    hits = jnp.sum(choose.astype(jnp.int32), axis=1)
    before = jnp.cumsum(hits, axis=0) - hits
    slot_index = jnp.sum(jnp.where(choose, before[:, None, :], 0), axis=2)
    slot_match = slot_index[:, :, None] == lax.broadcasted_iota(jnp.int32, (1, 1, CAP), 2)
    selector = jnp.einsum(
        "rke,rkc->ecr",
        choose.astype(jnp.bfloat16),
        slot_match.astype(jnp.bfloat16),
        preferred_element_type=jnp.float32,
    ).astype(jnp.bfloat16)
    whole_rows = lax.all_gather(narrow, "expert", axis=1, tiled=True)
    own_selector = lax.dynamic_slice_in_dim(
        selector, lax.axis_index("expert") * local_experts, local_experts, 0
    )
    outgoing = jnp.einsum(
        "ecr,rd->ecd", own_selector, whole_rows, preferred_element_type=jnp.float32
    ).astype(jnp.bfloat16)
    slab_rows = lax.all_gather(outgoing, "attn", axis=1, tiled=True)
    gate_part = jnp.einsum("end,edf->enf", slab_rows, w_gate, preferred_element_type=jnp.float32)
    up_part = jnp.einsum("end,edf->enf", slab_rows, w_up, preferred_element_type=jnp.float32)
    activation = (jax.nn.silu(gate_part) * up_part).astype(jnp.bfloat16)
    summed = lax.psum_scatter(
        jnp.einsum("enf,efd->ned", activation, w_down, preferred_element_type=jnp.float32).astype(
            jnp.bfloat16
        ),
        "attn",
        scatter_dimension=0,
        tiled=True,
    )
    expert_result = summed
    expert_result = expert_result.reshape(CAP, local_experts, expert_devices, width_local)
    returned = lax.all_to_all(expert_result, "expert", split_axis=2, concat_axis=1, tiled=True)
    flat_result = returned.reshape(CAP * E, width_local)
    target_index = slot_index * E + expert_ids
    picker = (
        target_index[:, :, None] == lax.broadcasted_iota(jnp.int32, (1, 1, CAP * E), 2)
    ).astype(jnp.bfloat16)
    taken = jnp.einsum("rkm,md->krd", picker, flat_result, preferred_element_type=jnp.float32)
    total = hidden_state + first_weight[:, None] * taken[0] + second_weight[:, None] * taken[1]
    return total.astype(jnp.bfloat16)


def solution(mesh):
    return jax.shard_map(
        on_device,
        mesh=mesh,
        in_specs=(
            P("attn", "expert"),
            P("attn", "expert"),
            P("attn", "expert", None, None),
            P("attn", "expert", None, None),
            P("attn", "expert"),
            P("attn", "expert"),
            P("attn"),
            P("expert"),
            P("expert", None),
            P("attn", None),
            P("expert", None, "attn"),
            P("expert", None, "attn"),
            P("expert", "attn", None),
        ),
        out_specs=P("attn", "expert"),
        check_vma=False,
    )
```

profile of v0, /device:TPU:0, one launch (start us, length us, event | category | flops | bytes accessed | tf_op | source)
XLA Modules:
  0.0 324.4 jit_solution(12968321372887208241)
XLA Ops:
  6.5 0.0 copy-start
  6.5 0.0 all-gather.2.cloned.1.call-start
  6.5 0.7 iota_compare_fusion.4
  7.3 0.8 copy.40
  8.1 0.2 convert_reduce_fusion
  8.2 0.1 reduce_window_sum.11
  8.3 1.2 select_reduce_fusion
  9.6 0.8 reshape.61
  10.4 0.8 reshape.55
  11.2 0.4 fusion.14
  11.6 1.2 reshape.50
  12.8 0.3 fusion.26
  13.0 0.0 copy-start.1
  13.0 4.6 %fusion.25 = (f32[64,2,6]{2,1,0:T(2,128)S(1)}, f32[64,2,6,128]{3,2,1,0:T(8,128)S(1)}) fusion(bf16[64,2,6,128]{3,2,1,0:T(8,128)(2,1)S(1)} %reshape.50, bf16[64,2,128,128]{3,2,1,0:T(8,128)(2,1)} %param.15, pred[64,128]{1,0:T(8,128)(4,1)S(1)} %iota_compare_fusion.4), kind=kOutput, calls=%fused_computation.51 | convolution fusion | flops 25459968 | bytes 4795392 | tf_op jit(solution)/shard_map/rkgd,rkld->rkgl/dot_general | solution.py:39
  17.7 0.0 copy-start.2
  17.7 0.1 fusion.18
  17.8 3.4 %convolution_add_fusion = f32[64,2,6,128]{3,2,1,0:T(8,128)S(1)} fusion(bf16[64,2,128,128]{3,2,1,0:T(8,128)(2,1)} %param.16, f32[64,2,6,128]{3,2,1,0:T(8,128)S(1)} %get-tuple-element.12, f32[64,2,128]{2,1,0:T(2,128)S(1)} %reshape.55, f32[64,2,6]{2,1,0:T(2,128)S(1)} %get-tuple-element.6, f32[64,2,6]{2,1,0:T(2,128)S(1)} %get-tuple-element.5), kind=kOutput, calls=%fused_computation.5 | convolution fusion | flops 25559040 | bytes 5052416 | tf_op jit(solution)/shard_map/rkgl,rkld->rkgd/dot_general | solution.py:57
  21.2 0.1 reshape.52
  21.3 0.0 copy-done.1
  21.3 0.2 multiply_reduce_fusion
  21.5 8.4 %psum.14 = f32[64]{0:T(128)S(1)} all-reduce(f32[64]{0:T(128)S(1)} %multiply_reduce_fusion), channel_id=1, replica_groups=mesh['attn'=8,'expert'=4] {'expert'}, use_global_device_ids=true, to_apply=%region_2.3 | all-reduce | flops 64 | bytes 512 | tf_op jit(solution)/shard_map/psum | solution.py:64
  29.9 0.0 copy-done.2
  29.9 0.1 fusion.9
  30.0 7.5 %all_gather.6 = bf16[64,6144]{1,0:T(8,128)(2,1)S(1)} all-gather(bf16[64,1536]{1,0:T(8,128)(2,1)S(1)} %fusion.9), channel_id=1, replica_groups=mesh['attn'=8,'expert'=4] {'expert'}, dimensions={1}, use_global_device_ids=true | all-gather | bytes 983040 | tf_op jit(solution)/shard_map/all_gather | solution.py:82
  37.5 1.3 convolution_convert_fusion.1
  38.8 0.0 all-gather.2.cloned.1.call-update
  38.8 0.2 reduce-scatter.2.cloned.1.call-start
  39.1 100.0 %all-gather.2.cloned.1.call-done = bf16[2,256,6144]{2,1,0:T(8,128)(2,1)} async-done(((bf16[2,32,6144]{2,1,0:T(8,128)(2,1)}), bf16[2,256,6144]{2,1,0:T(8,128)(2,1)}) %all-gather.2.cloned.1.call-update) | async-done | bytes 6291472 | tf_op jit(solution)/shard_map/all_gather | solution.py:89
  139.1 0.0 copy-start.4
  139.1 13.5 %fusion.27 = f32[2,256,1024]{2,1,0:T(8,128)S(1)} fusion(bf16[2,256,6144]{2,1,0:T(8,128)(2,1)} %all-gather.2.cloned.1.call-done, bf16[2,6144,1024]{2,1,0:T(8,128)(2,1)} %param.23), kind=kOutput, calls=%fused_computation.53 | convolution fusion | flops 6442450944 | bytes 33554432 | tf_op jit(solution)/shard_map/end,edf->enf/dot_general | solution.py:90
  152.6 0.0 copy-done.4
  152.6 12.3 %multiply_convert_fusion = bf16[2,256,1024]{2,1,0:T(8,128)(2,1)S(1)} fusion(f32[2,256,1024]{2,1,0:T(8,128)S(1)} %fusion.27, bf16[2,256,6144]{2,1,0:T(8,128)(2,1)S(1)} %copy-done.4, bf16[2,6144,1024]{2,1,0:T(8,128)(2,1)} %param.24), kind=kOutput, calls=%fused_computation.4 | convolution fusion | flops 6445596672 | bytes 34603008 | tf_op jit(solution)/shard_map/end,edf->enf/dot_general | solution.py:91
  164.9 16.8 %fusion = bf16[256,2,6144]{2,0,1:T(8,128)(2,1)} fusion(bf16[2,256,1024]{2,1,0:T(8,128)(2,1)S(1)} %multiply_convert_fusion, bf16[2,1024,6144]{2,1,0:T(8,128)(2,1)} %param.25), kind=kOutput, calls=%fused_computation.1 | convolution fusion | flops 6445596672 | bytes 32505856 | tf_op jit(solution)/shard_map/enf,efd->ned/dot_general | solution.py:94
  181.7 0.0 copy-start.3
  181.8 0.0 reduce-scatter.2.cloned.1.call-update
  181.8 0.1 copy.47
  181.8 0.0 copy-done
  181.8 0.5 fusion.10
  182.3 5.7 %psum.15 = f32[64,8]{0,1:T(8,128)S(1)} all-reduce(f32[64,8]{0,1:T(8,128)S(1)} %fusion.10), channel_id=1, replica_groups=mesh['attn'=8,'expert'=4] {'expert'}, use_global_device_ids=true, to_apply=%region_3.4 | all-reduce | flops 512 | bytes 4096 | tf_op jit(solution)/shard_map/psum | solution.py:66
  188.0 0.1 copy.41
  188.1 0.2 select_reduce_fusion.1
  188.3 109.8 %reduce-scatter.2.cloned.1.call-done = bf16[32,2,6144]{2,0,1:T(8,128)(2,1)} async-done(((bf16[256,2,6144]{2,0,1:T(8,128)(2,1)}), bf16[32,2,6144]{2,0,1:T(8,128)(2,1)}) %reduce-scatter.2.cloned.1.call-update) | async-done | bytes 786448 | tf_op jit(solution)/shard_map/reduce_scatter | solution.py:93
  298.1 2.1 copy.56
  300.2 3.5 %all-to-all-start = ((bf16[32,2,4,1536]{3,0,1,2:T(8,128)(2,1)}), bf16[32,2,4,1536]{3,0,1,2:T(8,128)(2,1)S(1)}, u32[]{:S(2)}, u32[]{:S(2)}) async-start(bf16[32,2,4,1536]{3,0,1,2:T(8,128)(2,1)} %bitcast.52), calls=%async_computation.1 | async-start | bytes 1572864 | tf_op jit(solution)/shard_map/all_to_all | solution.py:103
  303.7 0.1 fusion.24
  303.8 0.1 copy.50
  303.8 0.1 copy.51
  303.9 0.0 copy-done.3
  304.0 11.3 %all-to-all-done = bf16[32,2,4,1536]{3,0,1,2:T(8,128)(2,1)S(1)} async-done(((bf16[32,2,4,1536]{3,0,1,2:T(8,128)(2,1)}), bf16[32,2,4,1536]{3,0,1,2:T(8,128)(2,1)S(1)}, u32[]{:S(2)}, u32[]{:S(2)}) %all-to-all-start) | async-done | bytes 786464 | tf_op jit(solution)/shard_map/all_to_all | solution.py:103
  315.3 0.8 copy.46
  316.1 0.3 reshape.59
  316.4 0.3 convolution_bitcast_fusion
  316.7 0.8 fusion.6
  (5 shorter events, 0.1 us)
Async XLA Ops:
  6.5 175.3 %copy-start = (f32[1536,8]{0,1:T(8,128)S(1)}, f32[1536,8]{0,1:T(8,128)}, u32[]{:S(2)}) copy-start(f32[1536,8]{0,1:T(8,128)} %param.21) | copy-start | bytes 147460
  6.5 132.5 %all-gather.2.cloned.1.call-start = ((), (), s32[]{:S(2)}) async-start(), calls=%async_computation.2 | async-start | bytes 7077888 | tf_op jit(solution)/shard_map/all_gather | solution.py:89
  13.0 8.3 %copy-start.1 = (bf16[64,1536]{1,0:T(8,128)(2,1)S(1)}, bf16[64,1536]{1,0:T(8,128)(2,1)}, u32[]{:S(2)}) copy-start(bf16[64,1536]{1,0:T(8,128)(2,1)} %param.13) | copy-start | bytes 589828
  17.7 12.2 %copy-start.2 = (f32[1536]{0:T(1024)S(1)}, f32[1536]{0:T(1024)}, u32[]{:S(2)}) copy-start(f32[1536]{0:T(1024)} %param.20) | copy-start | bytes 18436
  38.8 259.3 %reduce-scatter.2.cloned.1.call-start = ((), (), s32[]{:S(2)}) async-start(), calls=%async_computation.3 | async-start | bytes 7077888 | tf_op jit(solution)/shard_map/reduce_scatter | solution.py:93
  139.1 13.6 %copy-start.4 = (bf16[2,256,6144]{2,1,0:T(8,128)(2,1)S(1)}, bf16[2,256,6144]{2,1,0:T(8,128)(2,1)}, u32[]{:S(2)}) copy-start(bf16[2,256,6144]{2,1,0:T(8,128)(2,1)} %all-gather.2.cloned.1.call-done) | copy-start | bytes 18874372
  181.7 122.2 %copy-start.3 = (s32[64,2]{0,1:T(2,128)S(1)}, s32[64,2]{0,1:T(2,128)}, u32[]{:S(2)}) copy-start(s32[64,2]{0,1:T(2,128)} %param.22) | copy-start | bytes 1540
  300.2 15.1 %all-to-all-start = ((bf16[32,2,4,1536]{3,0,1,2:T(8,128)(2,1)}), bf16[32,2,4,1536]{3,0,1,2:T(8,128)(2,1)S(1)}, u32[]{:S(2)}, u32[]{:S(2)}) async-start(bf16[32,2,4,1536]{3,0,1,2:T(8,128)(2,1)} %bitcast.52), calls=%async_computation.1 | async-start | bytes 1572864 | tf_op jit(solution)/shard_map/all_to_all | solution.py:103
Sparse Core Ops, SparseCore 0:
  39.0 100.0 all-gather.1
  181.9 116.1 reduce-scatter.1
where the time goes:
time: 325 us; the launch traced here: 324 us
  waiting for transfers between devices  221 us (68%)
  matrix products  53.5 us (16%)
  blocking collectives  21.5 us (7%)
  between operations  13.6 us (4%)
  local copies, waits for them, and re-layouts  7.22 us (2%)
  starting transfers between devices  3.72 us (1%)
  other arithmetic  3.66 us (1%)
    reduce_scatter x1, waiting for transfers between devices, on_device(): lax.psum_scatter(jnp.einsum('enf,efd->ned', activation, w_down, preferred...  110 us
    all_gather x1, waiting for transfers between devices, on_device(): slab_rows = lax.all_gather(outgoing, 'attn', axis=1, tiled=True)  100 us
    dot_general x1, matrix products, on_device(): jnp.einsum('enf,efd->ned', activation, w_down, preferred_element_type=jnp...  16.8 us
    dot_general x1, matrix products, on_device(): jnp.einsum('end,edf->enf', slab_rows, w_gate, preferred_element_type=jnp....  13.5 us
    dot_general x1, matrix products, on_device(): jnp.einsum('end,edf->enf', slab_rows, w_up, preferred_element_type=jnp.fl...  12.3 us
    all_to_all x1, waiting for transfers between devices, on_device(): lax.all_to_all(expert_result, 'expert', split_axis=2, concat_axis=1, tile...  11.3 us
    psum x1, blocking collectives, on_device(): lax.psum(jnp.sum(hidden_state * hidden_state, axis=1), 'expert')  8.4 us
    all_gather x1, blocking collectives, on_device(): whole_rows = lax.all_gather(narrow, 'expert', axis=1, tiled=True)  7.47 us
  transfers between devices with their start and end apart: 3, of which 3 were waited for; matrix products, arithmetic and copies ran while one was open for 0% of the time, Pallas kernels for 0%

commit v1 on v0

--- a/solution.py
+++ b/solution.py
@@ -86,7 +86,13 @@
     outgoing = jnp.einsum(
         "ecr,rd->ecd", own_selector, whole_rows, preferred_element_type=jnp.float32
     ).astype(jnp.bfloat16)
-    slab_rows = lax.all_gather(outgoing, "attn", axis=1, tiled=True)
+    size = lax.axis_size("attn")
+    held, blocks = (outgoing, [outgoing])
+    for _ in range(size - 1):
+        held = lax.ppermute(held, "attn", [(i, (i + 1) % size) for i in range(size)])
+        blocks.insert(0, held)
+    row_of_blocks = jnp.concatenate(blocks, axis=1)
+    slab_rows = jnp.roll(row_of_blocks, (lax.axis_index("attn") + 1) * outgoing.shape[1], axis=1)
     gate_part = jnp.einsum("end,edf->enf", slab_rows, w_gate, preferred_element_type=jnp.float32)
     up_part = jnp.einsum("end,edf->enf", slab_rows, w_up, preferred_element_type=jnp.float32)
     activation = (jax.nn.silu(gate_part) * up_part).astype(jnp.bfloat16)

time: 325 us -> 389 us (1.20)
  waiting for transfers between devices: 221 us -> 259 us
  local copies, waits for them, and re-layouts: 7.22 us -> 33.2 us
    ppermute x0 -> x7, waiting for transfers between devices: none -> 140 us  [on_device(): lax.ppermute(held, 'attn', [(i, (i + 1) % size) for i in range(size)])]
    all_gather x1 -> x0, waiting for transfers between devices: 100 us -> none  [on_device(): slab_rows = lax.all_gather(outgoing, 'attn', axis=1, tiled=True)]
    unnamed x13 -> x38, local copies, waits for them, and re-layouts: 0.94 us -> 25.9 us
  transfers between devices with their start and end apart: 3 -> 9, of which waited for: 3 -> 9; matrix products, arithmetic and copies ran while one was open for 0% -> 0% of each run, Pallas kernels for 0% -> 0%
where the time goes in v1:
time: 389 us; the launch traced here: 388 us
  waiting for transfers between devices  259 us (67%)
  matrix products  51.9 us (13%)
  local copies, waits for them, and re-layouts  33.2 us (9%)
  blocking collectives  21.5 us (6%)
  between operations  13.6 us (3%)
  starting transfers between devices  5.16 us (1%)
    ppermute x7, waiting for transfers between devices, on_device(): lax.ppermute(held, 'attn', [(i, (i + 1) % size) for i in range(size)])  140 us
    reduce_scatter x1, waiting for transfers between devices, on_device(): lax.psum_scatter(jnp.einsum('enf,efd->ned', activation, w_down, preferred...  108 us
    unnamed x38, local copies, waits for them, and re-layouts  25.9 us
    dot_general x1, matrix products, on_device(): jnp.einsum('end,edf->enf', slab_rows, w_gate, preferred_element_type=jnp....  14.4 us
    dot_general x1, matrix products, on_device(): jnp.einsum('enf,efd->ned', activation, w_down, preferred_element_type=jnp...  14.2 us
    dot_general x1, matrix products, on_device(): jnp.einsum('end,edf->enf', slab_rows, w_up, preferred_element_type=jnp.fl...  13.4 us
    all_to_all x1, waiting for transfers between devices, on_device(): lax.all_to_all(expert_result, 'expert', split_axis=2, concat_axis=1, tile...  11.3 us
    psum x1, blocking collectives, on_device(): lax.psum(jnp.sum(hidden_state * hidden_state, axis=1), 'expert')  8.39 us
  transfers between devices with their start and end apart: 9, of which 9 were waited for; matrix products, arithmetic and copies ran while one was open for 0% of the time, Pallas kernels for 0%

profile of v1, /device:TPU:0, one launch (start us, length us, event | category | flops | bytes accessed | tf_op | source)
XLA Modules:
  0.0 388.5 jit_solution(13765366494127515346)
XLA Ops:
  6.6 0.8 iota_compare_fusion.4
  7.3 0.8 copy.40
  8.1 0.2 convert_reduce_fusion
  8.3 0.1 reduce_window_sum.11
  8.4 1.2 select_reduce_fusion
  9.6 0.8 reshape.61
  10.4 0.8 reshape.55
  11.2 0.4 fusion.19
  11.6 1.2 reshape.50
  12.8 0.3 fusion.34
  13.1 4.6 %fusion.33 = (f32[64,2,6]{2,1,0:T(2,128)S(1)}, f32[64,2,6,128]{3,2,1,0:T(8,128)S(1)}) fusion(bf16[64,2,6,128]{3,2,1,0:T(8,128)(2,1)S(1)} %reshape.50, bf16[64,2,128,128]{3,2,1,0:T(8,128)(2,1)} %param.15, pred[64,128]{1,0:T(8,128)(4,1)S(1)} %iota_compare_fusion.4), kind=kOutput, calls=%fused_computation.75 | convolution fusion | flops 25459968 | bytes 4795392 | tf_op jit(solution)/shard_map/rkgd,rkld->rkgl/dot_general | solution.py:39
  17.7 0.1 fusion.23
  17.8 3.4 convolution_add_fusion
  21.2 0.1 reshape.52
  21.3 0.2 multiply_reduce_fusion
  21.5 8.4 %psum.14 = f32[64]{0:T(128)S(1)} all-reduce(f32[64]{0:T(128)S(1)} %multiply_reduce_fusion), channel_id=1, replica_groups=mesh['attn'=8,'expert'=4] {'expert'}, use_global_device_ids=true, to_apply=%region_2.3 | all-reduce | flops 64 | bytes 512 | tf_op jit(solution)/shard_map/psum | solution.py:64
  29.9 0.1 fusion.14
  30.0 7.5 %all_gather.3 = bf16[64,6144]{1,0:T(8,128)(2,1)S(1)} all-gather(bf16[64,1536]{1,0:T(8,128)(2,1)S(1)} %fusion.14), channel_id=1, replica_groups=mesh['attn'=8,'expert'=4] {'expert'}, dimensions={1}, use_global_device_ids=true | all-gather | bytes 983040 | tf_op jit(solution)/shard_map/all_gather | solution.py:82
  37.5 0.4 convolution_convert_fusion.1
  37.9 1.7 collective-permute-start
  39.5 21.1 %collective-permute-done = bf16[2,32,6144]{2,1,0:T(8,128)(2,1)S(1)} collective-permute-done((bf16[2,32,6144]{2,1,0:T(8,128)(2,1)S(1)}, bf16[2,32,6144]{2,1,0:T(8,128)(2,1)S(1)}, u32[]{:S(2)}, u32[]{:S(2)}) %collective-permute-start) | collective-permute-done | bytes 786464 | tf_op jit(solution)/shard_map/ppermute | solution.py:92
  60.7 21.8 %collective-permute-done.1 = bf16[2,32,6144]{2,1,0:T(8,128)(2,1)S(1)} collective-permute-done((bf16[2,32,6144]{2,1,0:T(8,128)(2,1)S(1)}, bf16[2,32,6144]{2,1,0:T(8,128)(2,1)S(1)}, u32[]{:S(2)}, u32[]{:S(2)}) %collective-permute-start.1) | collective-permute-done | bytes 786464 | tf_op jit(solution)/shard_map/ppermute | solution.py:92
  82.5 21.0 %collective-permute-done.2 = bf16[2,32,6144]{2,1,0:T(8,128)(2,1)S(1)} collective-permute-done((bf16[2,32,6144]{2,1,0:T(8,128)(2,1)S(1)}, bf16[2,32,6144]{2,1,0:T(8,128)(2,1)S(1)}, u32[]{:S(2)}, u32[]{:S(2)}) %collective-permute-start.2) | collective-permute-done | bytes 786464 | tf_op jit(solution)/shard_map/ppermute | solution.py:92
  103.5 0.9 copy-done.1
  104.4 20.1 %collective-permute-done.3 = bf16[2,32,6144]{2,1,0:T(8,128)(2,1)S(1)} collective-permute-done((bf16[2,32,6144]{2,1,0:T(8,128)(2,1)S(1)}, bf16[2,32,6144]{2,1,0:T(8,128)(2,1)S(1)}, u32[]{:S(2)}, u32[]{:S(2)}) %collective-permute-start.3) | collective-permute-done | bytes 786464 | tf_op jit(solution)/shard_map/ppermute | solution.py:92
  124.5 0.9 copy-done.3
  125.4 19.3 %collective-permute-done.4 = bf16[2,32,6144]{2,1,0:T(8,128)(2,1)S(1)} collective-permute-done((bf16[2,32,6144]{2,1,0:T(8,128)(2,1)S(1)}, bf16[2,32,6144]{2,1,0:T(8,128)(2,1)S(1)}, u32[]{:S(2)}, u32[]{:S(2)}) %collective-permute-start.4) | collective-permute-done | bytes 786464 | tf_op jit(solution)/shard_map/ppermute | solution.py:92
  144.7 0.9 copy-done.5
  145.6 18.5 %collective-permute-done.5 = bf16[2,32,6144]{2,1,0:T(8,128)(2,1)} collective-permute-done((bf16[2,32,6144]{2,1,0:T(8,128)(2,1)S(1)}, bf16[2,32,6144]{2,1,0:T(8,128)(2,1)}, u32[]{:S(2)}, u32[]{:S(2)}) %collective-permute-start.5) | collective-permute-done | bytes 786464 | tf_op jit(solution)/shard_map/ppermute | solution.py:92
  164.1 17.9 %collective-permute-done.6 = bf16[2,32,6144]{2,1,0:T(8,128)(2,1)} collective-permute-done((bf16[2,32,6144]{2,1,0:T(8,128)(2,1)}, bf16[2,32,6144]{2,1,0:T(8,128)(2,1)}, u32[]{:S(2)}, u32[]{:S(2)}) %collective-permute-start.6) | collective-permute-done | bytes 786464 | tf_op jit(solution)/shard_map/ppermute | solution.py:92
  182.0 2.1 constant_dynamic-update-slice_fusion.15
  184.0 2.1 constant_dynamic-update-slice_fusion.14
  186.1 2.1 constant_dynamic-update-slice_fusion.13
  188.2 2.1 constant_dynamic-update-slice_fusion.12
  190.3 2.1 constant_dynamic-update-slice_fusion.11
  192.4 1.0 constant_dynamic-update-slice_fusion.10
  193.4 1.0 constant_dynamic-update-slice_fusion.9
  194.3 1.0 constant_dynamic-update-slice_fusion.8
  195.3 2.1 constant_dynamic-update-slice_fusion.7
  197.4 2.1 constant_dynamic-update-slice_fusion.6
  199.5 0.9 constant_dynamic-update-slice_fusion.5
  200.4 1.0 constant_dynamic-update-slice_fusion.4
  201.4 1.0 constant_dynamic-update-slice_fusion.3
  202.4 1.0 constant_dynamic-update-slice_fusion.2
  203.4 0.9 constant_dynamic-update-slice_fusion.1
  204.3 1.0 constant_dynamic-update-slice_fusion
  205.3 13.4 %fusion.1 = f32[2,256,1024]{2,1,0:T(8,128)S(1)} fusion(bf16[2,6144,1024]{2,1,0:T(8,128)(2,1)} %param.24, bf16[2,512,6144]{2,1,0:T(8,128)(2,1)} %constant_dynamic-update-slice_fusion, s32[]{:T(128)S(6)} %select_n.33), kind=kOutput, calls=%fused_computation.3 | convolution fusion | flops 6442450944 | bytes 33554436 | tf_op jit(solution)/shard_map/end,edf->enf/dot_general | solution.py:97
  218.7 14.4 %fusion.3 = f32[2,256,1024]{2,1,0:T(8,128)} fusion(bf16[2,6144,1024]{2,1,0:T(8,128)(2,1)} %param.23, bf16[2,512,6144]{2,1,0:T(8,128)(2,1)} %constant_dynamic-update-slice_fusion, s32[]{:T(128)S(6)} %select_n.33), kind=kOutput, calls=%fused_computation.5 | convolution fusion | flops 6442450944 | bytes 33554436 | tf_op jit(solution)/shard_map/end,edf->enf/dot_general | solution.py:96
  233.1 14.2 %fusion = bf16[256,2,6144]{2,0,1:T(8,128)(2,1)} fusion(bf16[2,1024,6144]{2,1,0:T(8,128)(2,1)} %param.25, f32[2,256,1024]{2,1,0:T(8,128)S(1)} %fusion.1, f32[2,256,1024]{2,1,0:T(8,128)} %fusion.3), kind=kOutput, calls=%fused_computation.1 | convolution fusion | flops 6448742400 | bytes 35651584 | tf_op jit(solution)/shard_map/enf,efd->ned/dot_general | solution.py:100
  247.3 0.1 copy.47
  247.4 0.5 fusion.15
  247.9 5.7 %psum.15 = f32[64,8]{0,1:T(8,128)S(1)} all-reduce(f32[64,8]{0,1:T(8,128)S(1)} %fusion.15), channel_id=1, replica_groups=mesh['attn'=8,'expert'=4] {'expert'}, use_global_device_ids=true, to_apply=%region_3.4 | all-reduce | flops 512 | bytes 4096 | tf_op jit(solution)/shard_map/psum | solution.py:66
  253.5 0.1 copy.41
  253.6 0.2 select_reduce_fusion.1
  253.9 108.3 %reduce-scatter.2.cloned.1.call-done = bf16[32,2,6144]{2,0,1:T(8,128)(2,1)} async-done(((bf16[256,2,6144]{2,0,1:T(8,128)(2,1)}), bf16[32,2,6144]{2,0,1:T(8,128)(2,1)}) %reduce-scatter.2.cloned.1.call-update) | async-done | bytes 786448 | tf_op jit(solution)/shard_map/reduce_scatter | solution.py:99
  362.2 2.1 copy.56
  364.3 3.5 all-to-all-start
  367.8 0.1 fusion.32
  367.9 0.1 copy.50
  368.0 11.3 %all-to-all-done = bf16[32,2,4,1536]{3,0,1,2:T(8,128)(2,1)S(1)} async-done(((bf16[32,2,4,1536]{3,0,1,2:T(8,128)(2,1)}), bf16[32,2,4,1536]{3,0,1,2:T(8,128)(2,1)S(1)}, u32[]{:S(2)}, u32[]{:S(2)}) %all-to-all-start) | async-done | bytes 786464 | tf_op jit(solution)/shard_map/all_to_all | solution.py:109
  379.4 0.8 copy.46
  380.2 0.3 reshape.59
  380.5 0.3 convolution_bitcast_fusion
  380.8 0.8 fusion.11
  (31 shorter events, 0.2 us)
Async XLA Ops:
  6.5 240.9 %copy-start = (f32[1536,8]{0,1:T(8,128)S(1)}, f32[1536,8]{0,1:T(8,128)}, u32[]{:S(2)}) copy-start(f32[1536,8]{0,1:T(8,128)} %param.21) | copy-start | bytes 147460
  6.5 14.8 %copy-start.7 = (bf16[64,1536]{1,0:T(8,128)(2,1)S(1)}, bf16[64,1536]{1,0:T(8,128)(2,1)}, u32[]{:S(2)}) copy-start(bf16[64,1536]{1,0:T(8,128)(2,1)} %param.13) | copy-start | bytes 589828
  6.5 23.3 %copy-start.8 = (f32[1536]{0:T(1024)S(1)}, f32[1536]{0:T(1024)}, u32[]{:S(2)}) copy-start(f32[1536]{0:T(1024)} %param.20) | copy-start | bytes 18436
  6.5 355.7 %reduce-scatter.2.cloned.1.call-start = ((), (), s32[]{:S(2)}) async-start(), calls=%async_computation.2 | async-start | bytes 7077888 | tf_op jit(solution)/shard_map/reduce_scatter | solution.py:99
  37.9 22.8 %collective-permute-start = (bf16[2,32,6144]{2,1,0:T(8,128)(2,1)S(1)}, bf16[2,32,6144]{2,1,0:T(8,128)(2,1)S(1)}, u32[]{:S(2)}, u32[]{:S(2)}) collective-permute-start(bf16[2,32,6144]{2,1,0:T(8,128)(2,1)S(1)} %convolution_convert_fusion.1), channel_id=1, source_target_pairs={{0,4},{4,8},{8,12},{12,16},{16,20},{20,24},{24,28},{28,0},{1,5},{5... | collective-permute-start | bytes 2359304 | tf_op jit(solution)/shard_map/ppermute | solution.py:92
  60.6 21.8 %collective-permute-start.1 = (bf16[2,32,6144]{2,1,0:T(8,128)(2,1)S(1)}, bf16[2,32,6144]{2,1,0:T(8,128)(2,1)S(1)}, u32[]{:S(2)}, u32[]{:S(2)}) collective-permute-start(bf16[2,32,6144]{2,1,0:T(8,128)(2,1)S(1)} %collective-permute-done), channel_id=1, source_target_pairs={{0,4},{4,8},{8,12},{12,16},{16,20},{20,24},{24,28},{28,0},{1,5},{5... | collective-permute-start | bytes 2359304 | tf_op jit(solution)/shard_map/ppermute | solution.py:92
  82.5 21.0 %collective-permute-start.2 = (bf16[2,32,6144]{2,1,0:T(8,128)(2,1)S(1)}, bf16[2,32,6144]{2,1,0:T(8,128)(2,1)S(1)}, u32[]{:S(2)}, u32[]{:S(2)}) collective-permute-start(bf16[2,32,6144]{2,1,0:T(8,128)(2,1)S(1)} %collective-permute-done.1), channel_id=1, source_target_pairs={{0,4},{4,8},{8,12},{12,16},{16,20},{20,24},{24,28},{28,0},{1,5},{5... | collective-permute-start | bytes 2359304 | tf_op jit(solution)/shard_map/ppermute | solution.py:92
  103.5 0.9 copy-start.1
  104.4 20.1 %collective-permute-start.3 = (bf16[2,32,6144]{2,1,0:T(8,128)(2,1)S(1)}, bf16[2,32,6144]{2,1,0:T(8,128)(2,1)S(1)}, u32[]{:S(2)}, u32[]{:S(2)}) collective-permute-start(bf16[2,32,6144]{2,1,0:T(8,128)(2,1)S(1)} %collective-permute-done.2), channel_id=1, source_target_pairs={{0,4},{4,8},{8,12},{12,16},{16,20},{20,24},{24,28},{28,0},{1,5},{5... | collective-permute-start | bytes 2359304 | tf_op jit(solution)/shard_map/ppermute | solution.py:92
  124.5 0.9 copy-start.3
  125.4 19.3 %collective-permute-start.4 = (bf16[2,32,6144]{2,1,0:T(8,128)(2,1)S(1)}, bf16[2,32,6144]{2,1,0:T(8,128)(2,1)S(1)}, u32[]{:S(2)}, u32[]{:S(2)}) collective-permute-start(bf16[2,32,6144]{2,1,0:T(8,128)(2,1)S(1)} %collective-permute-done.3), channel_id=1, source_target_pairs={{0,4},{4,8},{8,12},{12,16},{16,20},{20,24},{24,28},{28,0},{1,5},{5... | collective-permute-start | bytes 2359304 | tf_op jit(solution)/shard_map/ppermute | solution.py:92
  144.7 0.9 copy-start.5
  145.6 18.5 %collective-permute-start.5 = (bf16[2,32,6144]{2,1,0:T(8,128)(2,1)S(1)}, bf16[2,32,6144]{2,1,0:T(8,128)(2,1)}, u32[]{:S(2)}, u32[]{:S(2)}) collective-permute-start(bf16[2,32,6144]{2,1,0:T(8,128)(2,1)S(1)} %collective-permute-done.4), channel_id=1, source_target_pairs={{0,4},{4,8},{8,12},{12,16},{16,20},{20,24},{24,28},{28,0},{1,5},{5... | collective-permute-start | bytes 2359304 | tf_op jit(solution)/shard_map/ppermute | solution.py:92
  164.1 17.9 %collective-permute-start.6 = (bf16[2,32,6144]{2,1,0:T(8,128)(2,1)}, bf16[2,32,6144]{2,1,0:T(8,128)(2,1)}, u32[]{:S(2)}, u32[]{:S(2)}) collective-permute-start(bf16[2,32,6144]{2,1,0:T(8,128)(2,1)} %collective-permute-done.5), channel_id=1, source_target_pairs={{0,4},{4,8},{8,12},{12,16},{16,20},{20,24},{24,28},{28,0},{1,5},{5... | collective-permute-start | bytes 2359304 | tf_op jit(solution)/shard_map/ppermute | solution.py:92
  164.1 35.4 %copy-start.6 = (bf16[2,32,6144]{2,1,0:T(8,128)(2,1)S(1)}, bf16[2,32,6144]{2,1,0:T(8,128)(2,1)}, u32[]{:S(2)}) copy-start(bf16[2,32,6144]{2,1,0:T(8,128)(2,1)} %copy-done.5) | copy-start | bytes 2359300
  164.1 36.3 %copy-start.4 = (bf16[2,32,6144]{2,1,0:T(8,128)(2,1)S(1)}, bf16[2,32,6144]{2,1,0:T(8,128)(2,1)}, u32[]{:S(2)}) copy-start(bf16[2,32,6144]{2,1,0:T(8,128)(2,1)} %copy-done.3) | copy-start | bytes 2359300
  164.1 37.3 %copy-start.2 = (bf16[2,32,6144]{2,1,0:T(8,128)(2,1)S(1)}, bf16[2,32,6144]{2,1,0:T(8,128)(2,1)}, u32[]{:S(2)}) copy-start(bf16[2,32,6144]{2,1,0:T(8,128)(2,1)} %copy-done.1) | copy-start | bytes 2359300
  233.1 134.9 %copy-start.9 = (s32[64,2]{0,1:T(2,128)S(1)}, s32[64,2]{0,1:T(2,128)}, u32[]{:S(2)}) copy-start(s32[64,2]{0,1:T(2,128)} %param.22) | copy-start | bytes 1540
  364.3 15.1 %all-to-all-start = ((bf16[32,2,4,1536]{3,0,1,2:T(8,128)(2,1)}), bf16[32,2,4,1536]{3,0,1,2:T(8,128)(2,1)S(1)}, u32[]{:S(2)}, u32[]{:S(2)}) async-start(bf16[32,2,4,1536]{3,0,1,2:T(8,128)(2,1)} %bitcast.49), calls=%async_computation.1 | async-start | bytes 1572864 | tf_op jit(solution)/shard_map/all_to_all | solution.py:109
Sparse Core Ops, SparseCore 0:
  247.4 114.7 reduce-scatter.1
